TPU v7x, 256 devices: a whole 4x4x8 slice. The times are simulated.
256 devices in a mesh: sub: 8 (over y, z_lo), row: 16 (over x, z_hi), col: 2 (over core).
Axes of the slice: x: 4, y: 4, z: 8 (z_hi: 4, z_lo: 2; z = z_hi * 2 + z_lo), core: 2. Of those that a mesh axis runs over, the one named last changes fastest.
Arguments:
- child_pivot: float32 [8, 1024, 1024], P('sub', 'row'), as said below
- child_border: float32 [8, 4096, 1024], P('sub', 'row'), as said below
- child_update: float32 [8, 4096, 4096], P('sub', 'row', 'col'), as said below
- parent_front: float32 [16384, 16384], P('row', ('sub', 'col')), as said below
- tile_map: int32 [8, 32], replicated, may hold values from -1 to 127, as said below
Outputs:
- schur_block: float32 [16384, 16384], P('row', ('sub', 'col'))
- panel_rows: float32 [16384, 256], P('row')
Inputs may be any that keep to these rules, and one draw needn't show every extreme that they name: For each child s the matrix [[child_pivot[s], child_border[s]^T], [child_border[s], child_update[s]]] is symmetric positive definite; child_pivot[s] and child_update[s] are symmetric. `child_border`: see child_pivot: the border of a symmetric positive definite child front. `child_update`: see child_pivot: the trailing block of a symmetric positive definite child front. `parent_front`: symmetric positive definite. tile_map[s, t] is the parent tile that receives tile t of child s, or -1 where t lies beyond child s's front; the -1 entries of a child come after its live ones, every child has 16 live tiles or more, some child has all 32 live and some exactly 16; the live entries of one child are distinct; the child tiles t with t // 2 == i map into parent tiles i * 8 to (i + 1) * 8 - 1.
All inputs are finite; a program needn't handle non-finite values.
Results may differ from a plain program's by a relative error of at most 0.0001.
Values sent between devices are 32-bit elements; how exact they have to be, the bound alone decides.
No kernel may reach another device: no remote copies, remote signals or barrier semaphores. Data moves between devices by JAX's collectives and lax.ppermute only.
A program may use at most 128 MiB of HBM per device.

v0:
```python
import jax
import jax.numpy as jnp
from jax import lax
from jax.sharding import PartitionSpec as P

PANEL = 256
TILE = 128


highest = lax.Precision.HIGHEST


def picked(value, axis, root):
    return lax.dynamic_index_in_dim(lax.all_gather(value, axis), root, 0, keepdims=False)


def filled_up(lines, peers):
    spare = -len(lines) % peers
    return jnp.pad(lines, [(0, spare)] + [(0, 0)] * (lines.ndim - 1))


def spread(value, axis, root):
    lines = jnp.where(lax.axis_index(axis) == root, value, jnp.zeros_like(value)).reshape(
        -1, *value.shape[1:][-1:]
    )
    padded = filled_up(lines, lax.axis_size(axis))
    own = lax.psum_scatter(padded, axis, scatter_dimension=0, tiled=True)
    return lax.all_gather(own, axis, axis=0, tiled=True)[: len(lines)].reshape(value.shape)


def solve_rows(lower_tri, right_rows):
    return jax.scipy.linalg.solve_triangular(lower_tri, right_rows.T, lower=True).T


def onehot_tiles(tile_ids, first_tile, width):
    local_ids = tile_ids - first_tile
    return (local_ids[:, :, None] == jnp.arange(width, dtype=jnp.int32)[None, None, :]).astype(
        jnp.float32
    )


def on_device(child_pivot, child_border, child_update, parent_front, tile_map):
    sub_count = lax.axis_size("sub")
    column_count = lax.axis_size("col")
    row_index = lax.axis_index("row")
    column_index = lax.axis_index("col")
    my_group = lax.axis_index("sub") * column_count + column_index
    local_rows = child_update.shape[1]
    half_cols = child_update.shape[2]
    group_width = half_cols // sub_count
    pivot_full = lax.all_gather(child_pivot[0], "row", axis=0, tiled=True)
    border_local = child_border[0]
    all_border = lax.all_gather(border_local, "row", axis=0, tiled=True)
    lower_tri = jnp.linalg.cholesky(pivot_full)
    own_factor = solve_rows(lower_tri, border_local)
    far_border = lax.dynamic_slice_in_dim(all_border, column_index * half_cols, half_cols, 0)
    far_factor = solve_rows(lower_tri, far_border)
    contrib = child_update[0] - jnp.dot(
        own_factor, far_factor.T, precision=highest, preferred_element_type=jnp.float32
    )
    shaped = contrib.reshape(local_rows, sub_count // column_count, column_count, group_width)
    first_step = lax.all_to_all(shaped, "col", split_axis=2, concat_axis=1, tiled=True)
    second_step = lax.all_to_all(
        first_step.reshape(local_rows, sub_count, group_width),
        "sub",
        split_axis=1,
        concat_axis=0,
        tiled=True,
    )
    arrived = second_step.reshape(sub_count, local_rows, group_width)
    row_tiles = local_rows // TILE
    group_tiles = group_width // TILE
    parent_rows = parent_front.shape[0]
    parent_cols = parent_front.shape[1]
    tile_rows = lax.dynamic_slice_in_dim(tile_map, row_index * row_tiles, row_tiles, 1)
    tile_cols = lax.dynamic_slice_in_dim(tile_map, my_group * group_tiles, group_tiles, 1)
    row_onehot = onehot_tiles(tile_rows, row_index * (parent_rows // TILE), parent_rows // TILE)
    column_onehot = onehot_tiles(tile_cols, my_group * (parent_cols // TILE), parent_cols // TILE)
    blocks = arrived.reshape(sub_count, row_tiles, TILE, group_tiles, TILE)
    placed = jnp.einsum("skb,sixkz->sixbz", column_onehot, blocks, precision=highest)
    assembled = jnp.einsum("sia,sixbz->axbz", row_onehot, placed, precision=highest)
    parent = parent_front + assembled.reshape(parent_rows, parent_cols)
    group_zero = picked(parent[:, :PANEL], ("sub", "col"), 0)
    top_block = picked(group_zero[:PANEL], "row", 0)
    top_lower = jnp.linalg.cholesky(top_block)
    panel_rows = solve_rows(top_lower, group_zero)
    per_group = parent_cols // parent_rows
    pieces = spread(panel_rows, "row", my_group * per_group + 0)
    schur_block = parent - jnp.dot(
        panel_rows, pieces.T, precision=highest, preferred_element_type=jnp.float32
    )
    return (schur_block, panel_rows)


def solution(mesh):
    placed = (
        P("sub", "row", None),
        P("sub", "row", None),
        P("sub", "row", "col"),
        P("row", ("sub", "col")),
        P(),
    )
    return jax.shard_map(
        on_device,
        mesh=mesh,
        in_specs=placed,
        out_specs=(P("row", ("sub", "col")), P("row", None)),
        check_vma=False,
    )
```

profile of v0, /device:TPU:8, one launch (start us, length us, event | category | flops | bytes accessed | tf_op | source)
XLA Modules:
  0.0 982.7 jit_solution(8342023569343779837)
XLA Ops:
  11.5 77.5 %all-gather.13.cloned.1.call-done = f32[1,1024,1024]{2,0,1:T(1,128)} async-done(((f32[1,64,1024]{2,0,1:T(1,128)}), f32[1,1024,1024]{2,0,1:T(1,128)}) %all-gather.13.cloned.1.call-update) | async-done | bytes 4194320 | tf_op jit(solution)/shard_map/all_gather | solution.py:51
  89.0 10.9 %copy.26 = f32[1,1024,1024]{1,2,0:T(8,128)} copy(f32[1,1024,1024]{2,0,1:T(1,128)} %all-gather.13.cloned.1.call-done) | data formatting | bytes 8388608 | tf_op jit(solution)/shard_map/all_gather | solution.py:51
  106.8 11.7 %cholesky.250 = f32[128,128]{1,0:T(8,128)S(1)} custom-call(f32[128,128]{1,0:T(8,128)S(1)} %cholesky.653), custom_call_target="Cholesky" | custom-call | tf_op jit(solution)/shard_map/jit(cholesky)/cholesky | solution.py:54
  118.6 9.8 custom-call.74
  134.8 11.8 %cholesky.275 = f32[128,128]{1,0:T(8,128)S(1)} custom-call(f32[128,128]{1,0:T(8,128)S(1)} %cholesky.657), custom_call_target="Cholesky" | custom-call | tf_op jit(solution)/shard_map/jit(cholesky)/cholesky | solution.py:54
  160.4 11.7 %cholesky.300 = f32[128,128]{1,0:T(8,128)S(1)} custom-call(f32[128,128]{1,0:T(8,128)S(1)} %cholesky.662), custom_call_target="Cholesky" | custom-call | tf_op jit(solution)/shard_map/jit(cholesky)/cholesky | solution.py:54
  186.1 11.9 %cholesky.541 = f32[128,128]{1,0:T(8,128)S(1)} custom-call(f32[128,128]{1,0:T(8,128)S(1)} %cholesky.667), custom_call_target="Cholesky" | custom-call | tf_op jit(solution)/shard_map/jit(cholesky)/cholesky | solution.py:54
  211.9 11.7 %cholesky.560 = f32[128,128]{1,0:T(8,128)S(1)} custom-call(f32[128,128]{1,0:T(8,128)S(1)} %cholesky.672), custom_call_target="Cholesky" | custom-call | tf_op jit(solution)/shard_map/jit(cholesky)/cholesky | solution.py:54
  224.2 10.2 %custom-call.78 = f32[1,128,128]{1,2,0:T(8,128)S(1)} custom-call(f32[1,128,128]{2,1,0:T(8,128)S(1)} %get-tuple-element.108), custom_call_target="InvertDiagBlocksLowerTriangular" | custom-call | tf_op jit(solution)/shard_map/jit(cholesky)/cholesky | solution.py:54
  237.8 11.7 %cholesky.580 = f32[128,128]{1,0:T(8,128)S(1)} custom-call(f32[128,128]{1,0:T(8,128)S(1)} %cholesky.677), custom_call_target="Cholesky" | custom-call | tf_op jit(solution)/shard_map/jit(cholesky)/cholesky | solution.py:54
  262.9 11.9 %cholesky.600 = f32[128,128]{1,0:T(8,128)S(1)} custom-call(f32[128,128]{1,0:T(8,128)S(1)} %cholesky.682), custom_call_target="Cholesky" | custom-call | tf_op jit(solution)/shard_map/jit(cholesky)/cholesky | solution.py:54
  287.9 11.7 %cholesky.614 = f32[128,128]{1,0:T(8,128)S(1)} custom-call(f32[128,128]{1,0:T(8,128)S(1)} %convolution_subtract_fusion.22), custom_call_target="Cholesky" | custom-call | tf_op jit(solution)/shard_map/jit(cholesky)/cholesky | solution.py:54
  314.9 24.1 %while.2 = (s32[]{:T(128)}, f32[1024,1024]{1,0:T(8,128)}, s32[8,2]{0,1:T(2,128)S(1)}, f32[8,128,128]{2,1,0:T(8,128)S(1)}, s32[]{:T(128)}) while((s32[]{:T(128)}, f32[1024,1024]{1,0:T(8,128)}, s32[8,2]{0,1:T(2,128)S(1)}, f32[8,128,128]{2,1,0:T(8,128)S(1)}, s32[]{:T(128)}) %tuple.105), condition=%wide.while_cond, body=%wide.while_body.sunk | while | flops 2 | bytes 131181 | solution.py:32
  339.0 78.6 %custom-call.80 = f32[8,128,128]{1,2,0:T(8,128)S(1)} custom-call(f32[8,128,128]{2,1,0:T(8,128)S(1)} %get-tuple-element.10), custom_call_target="InvertDiagBlocksLowerTriangular" | custom-call | tf_op jit(solution)/shard_map/jit(_solve_triangular)/triangular_solve | solution.py:32
  520.7 19.6 %all-to-all-done.1 = f32[256,8,256]{2,0,1:T(8,128)S(1)} async-done(((f32[256,8,256]{2,0,1:T(8,128)}), f32[256,8,256]{2,0,1:T(8,128)S(1)}, u32[]{:S(2)}, u32[]{:S(2)}) %all-to-all-start.1) | async-done | bytes 2097184 | tf_op jit(solution)/shard_map/all_to_all | solution.py:63
  570.0 91.1 %all-gather.17.cloned.1.call-done = f32[16384,256]{0,1:T(8,128)} async-done(((f32[1024,256]{0,1:T(8,128)}), f32[16384,256]{0,1:T(8,128)}) %all-gather.17.cloned.1.call-update) | async-done | bytes 16777232 | tf_op jit(solution)/shard_map/all_gather | solution.py:14
  661.1 17.5 %copy.36 = f32[16384,256]{1,0:T(8,128)} copy(f32[16384,256]{0,1:T(8,128)} %all-gather.17.cloned.1.call-done) | data formatting | bytes 33554432 | tf_op jit(solution)/shard_map/all_gather | solution.py:14
  681.8 74.7 %all-gather.9.cloned.1.call-done = f32[16,256,256]{2,1,0:T(8,128)} async-done(((f32[1,256,256]{2,1,0:T(8,128)}), f32[16,256,256]{2,1,0:T(8,128)}) %all-gather.9.cloned.1.call-update) | async-done | bytes 4194320 | tf_op jit(solution)/shard_map/all_gather | solution.py:14
  758.6 11.7 %cholesky.628 = f32[128,128]{1,0:T(8,128)S(1)} custom-call(f32[128,128]{1,0:T(8,128)S(1)} %cholesky.686), custom_call_target="Cholesky" | custom-call | tf_op jit(solution)/shard_map/jit(cholesky)/cholesky | solution.py:85
  770.4 9.8 custom-call.84
  780.7 11.7 %cholesky.637 = f32[128,128]{1,0:T(8,128)S(1)} custom-call(f32[128,128]{1,0:T(8,128)S(1)} %convolution_subtract_fusion.21), custom_call_target="Cholesky" | custom-call | tf_op jit(solution)/shard_map/jit(cholesky)/cholesky | solution.py:85
  799.0 19.7 %custom-call.81 = f32[2,128,128]{1,2,0:T(8,128)S(1)} custom-call(f32[2,128,128]{2,1,0:T(8,128)S(1)} %get-tuple-element.18), custom_call_target="InvertDiagBlocksLowerTriangular" | custom-call | tf_op jit(solution)/shard_map/jit(_solve_triangular)/triangular_solve | solution.py:32
  822.1 87.8 %reduce-scatter.4.cloned.1.call-done = f32[64,256]{1,0:T(8,128)} async-done(((f32[1024,256]{1,0:T(8,128)}), f32[64,256]{1,0:T(8,128)}) %reduce-scatter.4.cloned.1.call-update) | async-done | bytes 65552 | tf_op jit(solution)/shard_map/reduce_scatter | solution.py:27
  911.3 52.1 %all-gather.11.cloned.1.call-done = f32[1024,256]{1,0:T(8,128)} async-done(((f32[64,256]{1,0:T(8,128)}), f32[1024,256]{1,0:T(8,128)}) %all-gather.11.cloned.1.call-update) | async-done | bytes 1048592 | tf_op jit(solution)/shard_map/all_gather | solution.py:28
  (184 shorter events, 288.0 us)
Async XLA Ops:
  7.2 81.8 %all-gather.13.cloned.1.call-start = ((), (), s32[]{:S(2)}) async-start(), calls=%async_computation.5 | async-start | bytes 4456448 | tf_op jit(solution)/shard_map/all_gather | solution.py:51
  9.2 420.7 %all-gather.15.cloned.1.call-start = ((), (), s32[]{:S(2)}) async-start(), calls=%async_computation.6 | async-start | bytes 17825792 | tf_op jit(solution)/shard_map/all_gather | solution.py:53
  104.9 1.9 copy-start.1
  429.9 8.7 copy-start.4
  448.1 6.4 slice-start
  450.8 3.7 slice-start.1
  481.2 6.7 copy-start.3
  481.2 6.7 copy-start.5
  500.1 14.6 %copy-start.6 = (s32[8,32]{1,0:T(8,128)S(1)}, s32[8,32]{1,0:T(8,128)}, u32[]{:S(2)}) copy-start(s32[8,32]{1,0:T(8,128)} %param.11) | copy-start | bytes 3076
  506.5 33.8 %all-to-all-start.1 = ((f32[256,8,256]{2,0,1:T(8,128)}), f32[256,8,256]{2,0,1:T(8,128)S(1)}, u32[]{:S(2)}, u32[]{:S(2)}) async-start(f32[256,8,256]{2,0,1:T(8,128)} %bitcast.245), calls=%async_computation.1 | async-start | bytes 4194304 | tf_op jit(solution)/shard_map/all_to_all | solution.py:63
  514.8 146.3 %all-gather.17.cloned.1.call-start = ((), (), s32[]{:S(2)}) async-start(), calls=%async_computation.7 | async-start | bytes 17825792 | tf_op jit(solution)/shard_map/all_gather | solution.py:14
  540.3 1.3 copy-start.2
  566.8 2.0 copy-start
  569.9 186.6 %all-gather.9.cloned.1.call-start = ((), (), s32[]{:S(2)}) async-start(), calls=%async_computation.3 | async-start | bytes 4456448 | tf_op jit(solution)/shard_map/all_gather | solution.py:14
  680.2 229.7 %reduce-scatter.4.cloned.1.call-start = ((), (), s32[]{:S(2)}) async-start(), calls=%async_computation.8 | async-start | bytes 1114112 | tf_op jit(solution)/shard_map/reduce_scatter | solution.py:27
  822.0 141.4 %all-gather.11.cloned.1.call-start = ((), (), s32[]{:S(2)}) async-start(), calls=%async_computation.4 | async-start | bytes 1114112 | tf_op jit(solution)/shard_map/all_gather | solution.py:28
Sparse Core Ops, SparseCore 0:
  11.0 77.9 all-gather.12
  91.4 200.8 all-gather.14
  570.0 90.9 all-gather.16
  680.3 76.0 all-gather.8
  822.1 87.7 reduce-scatter.3
  912.2 51.1 all-gather.10
where the time goes:
time: 994 us; the launch traced here: 983 us
  waiting for transfers between devices  404 us (41%)
  other arithmetic  321 us (32%)
  local copies, waits for them, and re-layouts  116 us (12%)
  matrix products  105 us (11%)
  between operations  21.5 us (2%)
    another operation x30, other arithmetic, on_device(): lower_tri = jnp.linalg.cholesky(pivot_full)  172 us
    all_gather x2, waiting for transfers between devices, picked(): lax.all_gather(value, axis)  166 us
    another operation x6, other arithmetic, solve_rows(): jax.scipy.linalg.solve_triangular(lower_tri, right_rows.T, lower=True)  103 us
    reduce_scatter x1, waiting for transfers between devices, spread(): own = lax.psum_scatter(padded, axis, scatter_dimension=0, tiled=True)  87.8 us
    all_gather x1, waiting for transfers between devices, on_device(): pivot_full = lax.all_gather(child_pivot[0], 'row', axis=0, tiled=True)  77.5 us
    another operation x33, matrix products, solve_rows(): jax.scipy.linalg.solve_triangular(lower_tri, right_rows.T, lower=True)  53.5 us
    all_gather x1, waiting for transfers between devices, spread(): lax.all_gather(own, axis, axis=0, tiled=True)[:len(lines)]  52.1 us
    another operation x7, other arithmetic, on_device(): top_lower = jnp.linalg.cholesky(top_block)  34.6 us
  transfers between devices with their start and end apart: 7, of which 6 were waited for; matrix products, arithmetic and copies ran while one was open for 35% of the time, Pallas kernels for 0%

commit v1 on v0

v1 whole, which is shorter than its diff:
```python
import jax
import jax.numpy as jnp
from jax import lax
from jax.experimental import pallas as pl
from jax.experimental.pallas import tpu as pltpu
from jax.sharding import Mesh, PartitionSpec as P

PANEL = 256
TILE = 128
AXES = ("y", "zl", "x", "zh", "core")
SIZES = (4, 2, 4, 4, 2)
ROW = ("x", "zh")
GRP = ("y", "zl", "core")
SUB = ("y", "zl")
LANES = 128

highest = lax.Precision.HIGHEST
VMEM = pl.BlockSpec(memory_space=pltpu.VMEM)
SMEM = pl.BlockSpec(memory_space=pltpu.SMEM)


def dot(a, b, ca=1, cb=0):
    return lax.dot_general(
        a, b, (((ca,), (cb,)), ((), ())), precision=highest, preferred_element_type=jnp.float32
    )


def inverse_factor_rows(groups):
    count = len(groups)
    full = (8, LANES)
    lane = lax.broadcasted_iota(jnp.int32, full, 1)
    sublane = lax.broadcasted_iota(jnp.int32, full, 0)
    d = list(groups)
    out = [None] * count
    for g in range(count):
        base = 8 * g
        inside = (lane >= base) & (lane < base + 8)
        own = d[g]
        cols = [jnp.broadcast_to(own[:, base + q : base + q + 1], full) for q in range(8)]
        e = [[None] * 8 for _ in range(8)]
        for q in range(8):
            for i in range(q, 8):
                e[i][q] = jnp.broadcast_to(cols[q][i : i + 1, :], full)
        y = []
        for i in range(8):
            row = jnp.broadcast_to(own[i : i + 1, :], full)
            y.append(jnp.where(inside, jnp.where(lane == base + i, 1.0, 0.0), row))
        inv = [None] * 8
        low = [[None] * 8 for _ in range(8)]
        for p in range(8):
            inv[p] = 1.0 / e[p][p]
            for i in range(p + 1, 8):
                low[i][p] = e[i][p] * inv[p]
            for i in range(p + 1, 8):
                for j in range(p + 1, i + 1):
                    e[i][j] = e[i][j] - low[i][p] * e[j][p]
                y[i] = y[i] - low[i][p] * y[p]
        rows = y[0] * lax.rsqrt(e[0][0])
        for i in range(1, 8):
            rows = jnp.where(sublane == i, y[i] * lax.rsqrt(e[i][i]), rows)
        out[g] = jnp.where(lane <= sublane + base, rows, 0.0)
        if g == count - 1:
            break
        s = [y[i] * inv[i] for i in range(8)]
        for i in range(6, -1, -1):
            for p in range(i + 1, 8):
                s[i] = s[i] - low[p][i] * s[p]
        for r in range(g + 1, count):
            acc = jnp.where(inside, 0.0, d[r])
            for q in range(8):
                acc = acc - jnp.broadcast_to(d[r][:, base + q : base + q + 1], full) * s[q]
            d[r] = acc
    return out


def inverse_factor_kernel(p_ref, x_ref, block_ref):
    n = x_ref.shape[0]
    steps = n // LANES
    if len(p_ref.shape) == 2:
        x_ref[...] = p_ref[...]
    else:
        halves, pieces, rows, _ = p_ref.shape
        for h in range(halves):
            for i in range(pieces):
                start = (i * halves + h) * rows
                x_ref[start : start + rows, :] = p_ref[h, i]
    square = (LANES, LANES)
    eye = (
        lax.broadcasted_iota(jnp.int32, square, 0) == lax.broadcasted_iota(jnp.int32, square, 1)
    ).astype(jnp.float32)

    def step(k, carry):
        k0 = pl.multiple_of(k * LANES, LANES)
        here = pl.ds(k0, LANES)
        groups = [x_ref[pl.ds(k0 + 8 * r, 8), here] for r in range(LANES // 8)]
        for r, rows in enumerate(inverse_factor_rows(groups)):
            block_ref[8 * r : 8 * r + 8, :] = rows
        x_ref[here, here] = eye
        block = block_ref[...]
        scaled = dot(block, x_ref[here, :])
        solved = dot(block, scaled, 0, 0)
        x_ref[here, :] = scaled

        def update(r, inner):
            there = pl.ds(pl.multiple_of(r * LANES, LANES), LANES)
            below = x_ref[there, here]
            x_ref[there, here] = jnp.zeros(square, jnp.float32)
            x_ref[there, :] = x_ref[there, :] - dot(below, solved)
            return inner

        lax.fori_loop(k + 1, steps, update, 0)
        return carry

    lax.fori_loop(0, steps, step, 0)
    row = lax.broadcasted_iota(jnp.int32, (LANES, n), 0)
    column = lax.broadcasted_iota(jnp.int32, (LANES, n), 1)

    def finish(k, carry):
        k0 = pl.multiple_of(k * LANES, LANES)
        x_ref[pl.ds(k0, LANES), :] = jnp.where(column <= row + k0, x_ref[pl.ds(k0, LANES), :], 0.0)
        return carry

    lax.fori_loop(0, steps, finish, 0)


def inverse_factor(block, n):
    return pl.pallas_call(
        inverse_factor_kernel,
        out_shape=jax.ShapeDtypeStruct((n, n), jnp.float32),
        in_specs=[VMEM],
        out_specs=VMEM,
        scratch_shapes=[pltpu.VMEM((LANES, LANES), jnp.float32)],
        compiler_params=pltpu.CompilerParams(vmem_limit_bytes=24 * 2**20),
        cost_estimate=pl.CostEstimate(flops=2 * n**3 * 6, bytes_accessed=8 * n * n, transcendentals=0),
        name="inverse_factor",
    )(block)


def contrib_kernel(w_ref, border_ref, update_ref, out_ref):
    pair, tile, depth = border_ref.shape
    product = dot(w_ref[...], border_ref[...].reshape(pair * tile, depth), 1, 1)
    for h in range(pair):
        out_ref[h] = update_ref[h] - product[:, h * tile : (h + 1) * tile]


def contributions(w, border, update):
    count, tile, depth = border.shape
    rows = w.shape[0]
    pair = 2
    return pl.pallas_call(
        contrib_kernel,
        grid=(count // pair,),
        out_shape=jax.ShapeDtypeStruct((count, rows, tile), jnp.float32),
        in_specs=[
            pl.BlockSpec((rows, depth), lambda j: (0, 0)),
            pl.BlockSpec((pair, tile, depth), lambda j: (j, 0, 0)),
            pl.BlockSpec((pair, rows, tile), lambda j: (j, 0, 0)),
        ],
        out_specs=pl.BlockSpec((pair, rows, tile), lambda j: (j, 0, 0)),
        compiler_params=pltpu.CompilerParams(vmem_limit_bytes=24 * 2**20),
        name="contributions",
    )(w, border, update)


def near_kernel(map_ref, at_ref, got_ref, base_ref, out_ref):
    i = at_ref[0]
    offset = got_ref.shape[1] - 16
    out_ref[...] = base_ref[...]
    for s in range(map_ref.shape[0]):
        for c in range(2):
            cb = map_ref[s, c]
            for a in range(2):
                ra = map_ref[s, 2 * i + a]

                @pl.when((ra >= 0) & (cb >= 0) & (cb < PANEL // TILE))
                def _():
                    rows = pl.ds(pl.multiple_of((ra - 8 * i) * 8, 8), 8)
                    lanes = pl.ds(pl.multiple_of(cb * TILE, TILE), TILE)
                    piece = got_ref[2 * s + c, offset + 8 * a : offset + 8 * a + 8, :]
                    out_ref[rows, lanes] = out_ref[rows, lanes] + piece


def assemble_kernel(map_ref, at_ref, got_ref, parent_ref, out_ref):
    i = at_ref[0]
    g = at_ref[1]
    out_ref[...] = parent_ref[...]
    for s in range(map_ref.shape[0]):
        for c in range(2):
            cb = map_ref[s, 2 * g + c]
            for a in range(2):
                ra = map_ref[s, 2 * i + a]

                @pl.when((ra >= 0) & (cb >= 0))
                def _():
                    rows = pl.ds(pl.multiple_of((ra - 8 * i) * TILE, TILE), TILE)
                    lanes = pl.ds(pl.multiple_of((cb - 8 * g) * TILE, TILE), TILE)
                    piece = got_ref[2 * s + c, TILE * a : TILE * a + TILE, :]
                    out_ref[rows, lanes] = out_ref[rows, lanes] + piece


def placed_sum(kernel, name, tile_map, at, got, base):
    return pl.pallas_call(
        kernel,
        out_shape=jax.ShapeDtypeStruct(base.shape, jnp.float32),
        in_specs=[SMEM, SMEM, VMEM, VMEM],
        out_specs=VMEM,
        compiler_params=pltpu.CompilerParams(vmem_limit_bytes=24 * 2**20),
        name=name,
    )(tile_map, at, got, base)


def gathered(value, axis):
    peers = lax.axis_size(axis)
    copies = jnp.broadcast_to(value[None], (peers, *value.shape))
    return lax.all_to_all(copies, axis, 0, 0, tiled=True)


def transposed_pairs():
    pairs = []
    for r in range(16):
        for k in range(16):

            def flat(row, group):
                x, zh = divmod(row, 4)
                y, rest = divmod(group, 4)
                zl, core = divmod(rest, 2)
                return (((y * 2 + zl) * 4 + x) * 4 + zh) * 2 + core

            pairs.append((flat(r, k), flat(k, r)))
    return pairs


def slices_to_rows(slices):
    count, rows, cols = slices.shape
    tiles = rows // 8
    return slices.reshape(count, tiles, 8, cols).transpose(1, 0, 2, 3).reshape(count * rows, cols)


def rows_to_slices(rows, count):
    total, cols = rows.shape
    tiles = total // (8 * count)
    return rows.reshape(tiles, count, 8, cols).transpose(1, 0, 2, 3).reshape(count, tiles * 8, cols)


def on_device(child_pivot, child_border, child_update, parent_front, tile_map):
    core = lax.axis_index("core")
    row = lax.axis_index(ROW)
    group = lax.axis_index(GRP)
    at = jnp.stack([row, group]).astype(jnp.int32)
    border = child_border[0]

    part = lax.dynamic_slice_in_dim(child_pivot[0], core * 32, 32, 0)
    pivot = gathered(gathered(gathered(part, "zh"), "x"), "core")
    pivot = pivot.reshape(2, 16, 32, pivot.shape[-1])

    half = lax.dynamic_slice_in_dim(border, core * TILE, TILE, 0)
    far_border = lax.all_gather(half, ROW, axis=0, tiled=False)

    update = child_update[0].reshape(256, 8, 2, TILE).transpose(2, 1, 0, 3)
    update = lax.all_to_all(update, "core", 0, 0, tiled=True).reshape(16, 256, TILE)

    base = lax.all_to_all(rows_to_slices(parent_front[:, :PANEL], 16), GRP, 0, 0, tiled=True)[0]

    inverse = inverse_factor(pivot, pivot.shape[-1])
    solved = dot(dot(border, inverse, 1, 1), inverse)
    contrib = contributions(solved, far_border, update)
    send = jnp.concatenate([contrib, rows_to_slices(contrib[0], 16)], axis=1)
    got = lax.all_to_all(send, GRP, 0, 0, tiled=True)

    mine = placed_sum(near_kernel, "near", tile_map, at, got, base)
    top = gathered(gathered(mine[:16], "x")[0], "zh")[0]
    far = lax.ppermute(mine, AXES, transposed_pairs())
    both = gathered(jnp.concatenate([mine, top], axis=0), GRP)
    parent = placed_sum(assemble_kernel, "assemble", tile_map, at, got, parent_front)
    near = slices_to_rows(both[:, :64])
    top_block = slices_to_rows(both[:, 64:])
    far = gathered(gathered(far, "zh"), "x").reshape(16, 64, PANEL)
    far = slices_to_rows(far)

    top_inverse = inverse_factor(top_block, PANEL)
    panel_rows = dot(near, top_inverse, 1, 1)
    far_rows = dot(far, top_inverse, 1, 1)
    schur_block = parent - dot(panel_rows, far_rows, 1, 1)
    return (schur_block, panel_rows)


def solution(mesh):
    fine = Mesh(mesh.devices.reshape(SIZES), AXES)
    placed = (
        P(SUB, ROW, None),
        P(SUB, ROW, None),
        P(SUB, ROW, "core"),
        P(ROW, GRP),
        P(),
    )
    return jax.shard_map(
        on_device,
        mesh=fine,
        in_specs=placed,
        out_specs=(P(ROW, GRP), P(ROW, None)),
        check_vma=False,
    )
```

time: 994 us -> 377 us (0.38)
  other arithmetic: 321 us -> 1.6 us
  waiting for transfers between devices: 404 us -> 101 us
  Pallas kernels: 0 us -> 99 us
  matrix products: 105 us -> 14.5 us
  local copies, waits for them, and re-layouts: 116 us -> 29.8 us
  blocking collectives: 6.31 us -> 73.6 us
  starting transfers between devices: 8.69 us -> 38.6 us
    another operation x43 -> x1, other arithmetic: 310 us -> 0.07 us  [on_device(): at = jnp.stack([row, group]).astype(jnp.int32)]
    all_gather x5 -> x1, waiting for transfers between devices: 295 us -> 0.02 us  [on_device(): far_border = lax.all_gather(half, ROW, axis=0, tiled=False)]
    pallas_call x0 -> x5, Pallas kernels: none -> 99 us  [the longest x2 87.5 us: inverse_factor(): pl.pallas_call(inverse_factor_kernel, out_shape=jax.ShapeDtypeStruct((n,...]
    reduce_scatter x1 -> x0, waiting for transfers between devices: 87.8 us -> none  [spread(): own = lax.psum_scatter(padded, axis, scatter_dimension=0, tiled=True)]
    all_to_all x1 -> x7, waiting for transfers between devices: 19.6 us -> 98 us  [the longest x4 68.5 us: gathered(): return lax.all_to_all(copies, axis, 0, 0, tiled=True)]
    another operation x49 -> x0, matrix products: 76.9 us -> none  [the longest x33 53.5 us: solve_rows(): jax.scipy.linalg.solve_triangular(lower_tri, right_rows.T, lower=True)]
    all_to_all x1 -> x4, blocking collectives: 6.31 us -> 73.6 us  [gathered(): return lax.all_to_all(copies, axis, 0, 0, tiled=True)]
    all_gather x2 -> x0, local copies, waits for them, and re-layouts: 28.3 us -> none  [the longest x1 17.5 us: picked(): lax.all_gather(value, axis)]
  transfers between devices with their start and end apart: 7 -> 9, of which waited for: 6 -> 7; matrix products, arithmetic and copies ran while one was open for 35% -> 5% of each run, Pallas kernels for 0% -> 23%
where the time goes in v1:
time: 377 us; the launch traced here: 373 us
  waiting for transfers between devices  101 us (27%)
  Pallas kernels  99 us (26%)
  blocking collectives  73.6 us (20%)
  starting transfers between devices  38.6 us (10%)
  local copies, waits for them, and re-layouts  29.8 us (8%)
  matrix products  14.5 us (4%)
  between operations  14.3 us (4%)
    pallas_call x2, Pallas kernels, inverse_factor(): pl.pallas_call(inverse_factor_kernel, out_shape=jax.ShapeDtypeStruct((n,...  87.5 us
    all_to_all x4, blocking collectives, gathered(): return lax.all_to_all(copies, axis, 0, 0, tiled=True)  73.6 us
    all_to_all x4, waiting for transfers between devices, gathered(): return lax.all_to_all(copies, axis, 0, 0, tiled=True)  68.5 us
    all_to_all x1, waiting for transfers between devices, on_device(): got = lax.all_to_all(send, GRP, 0, 0, tiled=True)  26.7 us
    all_to_all x4, starting transfers between devices, gathered(): return lax.all_to_all(copies, axis, 0, 0, tiled=True)  19.2 us
    dot_general x5, matrix products, dot(): lax.dot_general(a, b, (((ca,), (cb,)), ((), ())), precision=highest, pref...  14.5 us
    unnamed x20, local copies, waits for them, and re-layouts  11.4 us
    pallas_call x1, Pallas kernels, contributions(): pl.pallas_call(contrib_kernel, grid=(count // pair,), out_shape=jax.Shape...  9.09 us
  transfers between devices with their start and end apart: 9, of which 7 were waited for; matrix products, arithmetic and copies ran while one was open for 5% of the time, Pallas kernels for 23%

profile of v1, /device:TPU:8, one launch (start us, length us, event | category | flops | bytes accessed | tf_op | source)
XLA Modules:
  0.0 372.9 jit_solution(386491792272545263)
XLA Ops:
  14.3 3.9 %all-to-all-start.3 = ((f32[2,8,256,128]{3,2,1,0:T(8,128)}), f32[2,8,256,128]{3,2,1,0:T(8,128)S(1)}, u32[]{:S(2)}, u32[]{:S(2)}) async-start(f32[2,8,256,128]{3,2,1,0:T(8,128)} %bitcast.57), calls=%async_computation.3 | async-start | bytes 4194304 | tf_op jit(solution)/shard_map/all_to_all | solution.py:260
  21.1 38.1 %all_to_all.55 = f32[4,32,1024]{2,1,0:T(8,128)S(1)} all-to-all(f32[4,32,1024]{2,1,0:T(8,128)S(1)} %broadcast_in_dim.21), channel_id=1, replica_groups=mesh['y'=4,'zl'=2,'x'=4,'zh'=4,'core'=2] {'zh'}, dimensions={0} | all-to-all | bytes 1048576 | tf_op jit(solution)/shard_map/all_to_all | solution.py:215
  60.8 4.5 %all-to-all-start.1 = ((f32[4,4,32,1024]{3,2,1,0:T(8,128)}), f32[4,4,32,1024]{3,2,1,0:T(8,128)}, u32[]{:S(2)}, u32[]{:S(2)}) async-start(f32[4,4,32,1024]{3,2,1,0:T(8,128)} %broadcast_in_dim.22), calls=%async_computation.1 | async-start | bytes 4194304 | tf_op jit(solution)/shard_map/all_to_all | solution.py:215
  67.6 45.2 %all-to-all-done.1 = f32[4,4,32,1024]{3,2,1,0:T(8,128)} async-done(((f32[4,4,32,1024]{3,2,1,0:T(8,128)}), f32[4,4,32,1024]{3,2,1,0:T(8,128)}, u32[]{:S(2)}, u32[]{:S(2)}) %all-to-all-start.1) | async-done | bytes 2097184 | tf_op jit(solution)/shard_map/all_to_all | solution.py:215
  115.2 8.2 %all_to_all.56 = f32[2,4,4,32,1024]{4,3,2,1,0:T(8,128)} all-to-all(f32[2,4,4,32,1024]{4,3,2,1,0:T(8,128)S(1)} %broadcast_in_dim.23), channel_id=1, replica_groups=mesh['y'=4,'zl'=2,'x'=4,'zh'=4,'core'=2] {'core'}, dimensions={0} | all-to-all | bytes 8388608 | tf_op jit(solution)/shard_map/all_to_all | solution.py:215
  123.4 5.9 %all-to-all-start.5 = ((f32[16,64,256]{2,1,0:T(8,128)}), f32[16,64,256]{2,1,0:T(8,128)}, u32[]{:S(2)}, u32[]{:S(2)}) async-start(f32[16,64,256]{2,1,0:T(8,128)} %bitcast.58), calls=%async_computation.5 | async-start | bytes 2097152 | tf_op jit(solution)/shard_map/all_to_all | solution.py:262
  131.5 73.5 %inverse_factor.2 = f32[1024,1024]{1,0:T(8,128)S(1)} custom-call(f32[2,16,32,1024]{3,2,1,0:T(8,128)S(1)} %bitcast.55), custom_call_target="tpu_custom_call" | custom-call | flops 12884901888 | bytes 8388608 | tf_op jit(solution)/shard_map/inverse_factor/pallas_call | solution.py:127
  205.0 3.5 fusion
  208.5 3.7 %fusion.2.w_ref = f32[256,1024]{1,0:T(8,128)S(1)} fusion(f32[1024,256]{1,0:T(8,128)S(1)} %fusion, f32[1024,1024]{1,0:T(8,128)S(1)} %inverse_factor.2), kind=kOutput, calls=%fused_computation.16 | convolution fusion | flops 3221225472 | bytes 6291456 | tf_op jit(solution)/shard_map/dot_general | solution.py:23
  212.3 3.4 copy-done.4
  215.7 9.1 %contributions.1 = f32[16,256,128]{2,1,0:T(8,128)S(1)} custom-call(f32[256,1024]{1,0:T(8,128)S(1)} %fusion.2.w_ref, f32[16,128,1024]{2,1,0:T(8,128)S(1)} %copy-done.4, f32[16,256,128]{2,1,0:T(8,128)S(1)} %bitcast.53), custom_call_target="tpu_custom_call" | custom-call | tf_op jit(solution)/shard_map/contributions/pallas_call | solution.py:150
  226.3 5.9 %all-to-all-start.4 = ((f32[16,272,128]{2,1,0:T(8,128)}), f32[16,272,128]{2,1,0:T(8,128)S(1)}, u32[]{:S(2)}, u32[]{:S(2)}) async-start(f32[16,272,128]{2,1,0:T(8,128)} %pad_maximum_fusion), calls=%async_computation.4 | async-start | bytes 4456448 | tf_op jit(solution)/shard_map/all_to_all | solution.py:268
  233.2 26.7 %all-to-all-done.4.got_ref = f32[16,272,128]{2,1,0:T(8,128)S(1)} async-done(((f32[16,272,128]{2,1,0:T(8,128)}), f32[16,272,128]{2,1,0:T(8,128)S(1)}, u32[]{:S(2)}, u32[]{:S(2)}) %all-to-all-start.4) | async-done | bytes 2228256 | tf_op jit(solution)/shard_map/all_to_all | solution.py:268
  260.8 8.1 %all_to_all.57 = f32[4,16,256]{2,1,0:T(8,128)S(1)} all-to-all(f32[4,16,256]{2,1,0:T(8,128)S(1)} %broadcast_in_dim.24), channel_id=1, replica_groups=mesh['y'=4,'zl'=2,'x'=4,'zh'=4,'core'=2] {'x'}, dimensions={0} | all-to-all | bytes 131072 | tf_op jit(solution)/shard_map/all_to_all | solution.py:215
  269.6 3.3 all-to-all-start.7
  272.8 3.6 collective-permute-start
  276.5 3.4 collective-permute-done
  281.0 19.2 %all_to_all.58 = f32[4,64,256]{2,1,0:T(8,128)S(1)} all-to-all(f32[4,64,256]{2,1,0:T(8,128)S(1)} %broadcast_in_dim.28), channel_id=1, replica_groups=mesh['y'=4,'zl'=2,'x'=4,'zh'=4,'core'=2] {'zh'}, dimensions={0} | all-to-all | bytes 524288 | tf_op jit(solution)/shard_map/all_to_all | solution.py:215
  301.3 6.1 %all-to-all-start.10 = ((f32[4,4,64,256]{3,2,1,0:T(8,128)}), f32[4,4,64,256]{3,2,1,0:T(8,128)S(1)}, u32[]{:S(2)}, u32[]{:S(2)}) async-start(f32[4,4,64,256]{3,2,1,0:T(8,128)} %broadcast_in_dim.29), calls=%async_computation.10 | async-start | bytes 2097152 | tf_op jit(solution)/shard_map/all_to_all | solution.py:215
  307.4 10.9 %all-to-all-done.10 = f32[4,4,64,256]{3,2,1,0:T(8,128)S(1)} async-done(((f32[4,4,64,256]{3,2,1,0:T(8,128)}), f32[4,4,64,256]{3,2,1,0:T(8,128)S(1)}, u32[]{:S(2)}, u32[]{:S(2)}) %all-to-all-start.10) | async-done | bytes 1048608 | tf_op jit(solution)/shard_map/all_to_all | solution.py:215
  319.5 5.3 %all-to-all-start.8 = ((f32[16,80,256]{2,1,0:T(8,128)}), f32[16,80,256]{2,1,0:T(8,128)}, u32[]{:S(2)}, u32[]{:S(2)}) async-start(f32[16,80,256]{2,1,0:T(8,128)} %broadcast_in_dim.27), calls=%async_computation.8 | async-start | bytes 2621440 | tf_op jit(solution)/shard_map/all_to_all | solution.py:215
  330.6 11.3 %all-to-all-done.8 = f32[16,80,256]{2,1,0:T(8,128)} async-done(((f32[16,80,256]{2,1,0:T(8,128)}), f32[16,80,256]{2,1,0:T(8,128)}, u32[]{:S(2)}, u32[]{:S(2)}) %all-to-all-start.8) | async-done | bytes 1310752 | tf_op jit(solution)/shard_map/all_to_all | solution.py:215
  344.3 13.9 %inverse_factor.3 = f32[256,256]{1,0:T(8,128)S(1)} custom-call(f32[256,256]{1,0:T(8,128)S(1)} %bitcast.56), custom_call_target="tpu_custom_call" | custom-call | flops 201326592 | bytes 524288 | tf_op jit(solution)/shard_map/inverse_factor/pallas_call | solution.py:127
  360.8 5.2 %convolution_subtract_fusion = f32[1024,1024]{1,0:T(8,128)} fusion(f32[1024,1024]{1,0:T(8,128)S(1)} %copy-done.3, f32[1024,256]{1,0:T(8,128)S(1)} %fusion.3, f32[1024,256]{1,0:T(8,128)S(1)} %fusion.4), kind=kOutput, calls=%fused_computation.1 | convolution fusion | flops 3222274048 | bytes 10485760 | tf_op jit(solution)/shard_map/dot_general | solution.py:23
  (58 shorter events, 36.6 us)
Async XLA Ops:
  7.2 1.2 copy-start
  7.2 205.1 %all-gather.2.cloned.1.call-start = ((), (), s32[]{:S(2)}) async-start(), calls=%async_computation.11 | async-start | bytes 8912896 | tf_op jit(solution)/shard_map/all_gather | solution.py:257
  14.3 3.9 %copy-start.9 = (f32[1,64,1024]{2,1,0:T(8,128)S(1)}, f32[1,64,1024]{2,1,0:T(8,128)}, u32[]{:S(2)}) copy-start(f32[1,64,1024]{2,1,0:T(8,128)} %param.5) | copy-start | bytes 786436
  14.3 6.8 %all-to-all-start.3 = ((f32[2,8,256,128]{3,2,1,0:T(8,128)}), f32[2,8,256,128]{3,2,1,0:T(8,128)S(1)}, u32[]{:S(2)}, u32[]{:S(2)}) async-start(f32[2,8,256,128]{3,2,1,0:T(8,128)} %bitcast.57), calls=%async_computation.3 | async-start | bytes 4194304 | tf_op jit(solution)/shard_map/all_to_all | solution.py:260
  60.8 52.1 %all-to-all-start.1 = ((f32[4,4,32,1024]{3,2,1,0:T(8,128)}), f32[4,4,32,1024]{3,2,1,0:T(8,128)}, u32[]{:S(2)}, u32[]{:S(2)}) async-start(f32[4,4,32,1024]{3,2,1,0:T(8,128)} %broadcast_in_dim.22), calls=%async_computation.1 | async-start | bytes 4194304 | tf_op jit(solution)/shard_map/all_to_all | solution.py:215
  65.3 1.2 slice-start
  123.4 102.9 %all-to-all-start.5 = ((f32[16,64,256]{2,1,0:T(8,128)}), f32[16,64,256]{2,1,0:T(8,128)}, u32[]{:S(2)}, u32[]{:S(2)}) async-start(f32[16,64,256]{2,1,0:T(8,128)} %bitcast.58), calls=%async_computation.5 | async-start | bytes 2097152 | tf_op jit(solution)/shard_map/all_to_all | solution.py:262
  129.3 2.2 copy-start.6
  212.3 3.4 copy-start.4
  226.3 33.5 %copy-start.7 = (s32[8,32]{1,0:T(8,128)S(1)}, s32[8,32]{1,0:T(8,128)}, u32[]{:S(2)}) copy-start(s32[8,32]{1,0:T(8,128)} %map_ref.3) | copy-start | bytes 3076
  226.3 33.5 %all-to-all-start.4 = ((f32[16,272,128]{2,1,0:T(8,128)}), f32[16,272,128]{2,1,0:T(8,128)S(1)}, u32[]{:S(2)}, u32[]{:S(2)}) async-start(f32[16,272,128]{2,1,0:T(8,128)} %pad_maximum_fusion), calls=%async_computation.4 | async-start | bytes 4456448 | tf_op jit(solution)/shard_map/all_to_all | solution.py:268
  269.6 11.5 %all-to-all-start.7 = ((f32[4,16,256]{2,1,0:T(8,128)}), f32[4,16,256]{2,1,0:T(8,128)S(1)}, u32[]{:S(2)}, u32[]{:S(2)}) async-start(f32[4,16,256]{2,1,0:T(8,128)} %broadcast_in_dim.26), calls=%async_computation.7 | async-start | bytes 131072 | tf_op jit(solution)/shard_map/all_to_all | solution.py:215
  272.8 7.1 %collective-permute-start = (f32[64,256]{1,0:T(8,128)S(1)}, f32[64,256]{1,0:T(8,128)S(1)}, u32[]{:S(2)}, u32[]{:S(2)}) collective-permute-start(f32[64,256]{1,0:T(8,128)S(1)} %near.1), channel_id=1, source_target_pairs={{0,0},{1,2},{32,4},{33,6},{64,8},{65,10},{96,12},{97,14},{128,16},... | collective-permute-start | bytes 196616 | tf_op jit(solution)/shard_map/ppermute | solution.py:272
  301.3 17.0 %all-to-all-start.10 = ((f32[4,4,64,256]{3,2,1,0:T(8,128)}), f32[4,4,64,256]{3,2,1,0:T(8,128)S(1)}, u32[]{:S(2)}, u32[]{:S(2)}) async-start(f32[4,4,64,256]{3,2,1,0:T(8,128)} %broadcast_in_dim.29), calls=%async_computation.10 | async-start | bytes 2097152 | tf_op jit(solution)/shard_map/all_to_all | solution.py:215
  319.5 22.4 %all-to-all-start.8 = ((f32[16,80,256]{2,1,0:T(8,128)}), f32[16,80,256]{2,1,0:T(8,128)}, u32[]{:S(2)}, u32[]{:S(2)}) async-start(f32[16,80,256]{2,1,0:T(8,128)} %broadcast_in_dim.27), calls=%async_computation.8 | async-start | bytes 2621440 | tf_op jit(solution)/shard_map/all_to_all | solution.py:215
  324.8 2.2 copy-start.5
  328.5 2.0 copy-start.2
  358.3 2.6 copy-start.3
  359.3 6.7 %copy-start.8 = (f32[1024,256]{1,0:T(8,128)}, f32[1024,256]{1,0:T(8,128)S(1)}, u32[]{:S(2)}) copy-start(f32[1024,256]{1,0:T(8,128)S(1)} %fusion.3) | copy-start | bytes 3145732
  360.8 5.2 %copy-start.1 = (f32[1,256,1024]{2,1,0:T(8,128)S(1)}, f32[1,256,1024]{2,1,0:T(8,128)}, u32[]{:S(2)}) copy-start(f32[1,256,1024]{2,1,0:T(8,128)} %param.6) | copy-start | bytes 3145732
Sparse Core Ops, SparseCore 0:
  10.4 133.4 all-gather.1
